TPU v7x, 256 devices: a whole 4x4x8 slice. The times are simulated.
256 devices in a mesh: dp: 2 (over z_lo), seq: 32 (over y, x, core), head: 4 (over z_hi).
Axes of the slice: x: 4, y: 4, z: 8 (z_hi: 4, z_lo: 2; z = z_hi * 2 + z_lo), core: 2. Of those that a mesh axis runs over, the one named last changes fastest.
Arguments:
- x_in: bfloat16 [2, 24576, 4096], P('dp', 'seq', 'head'), may hold values from -6 to 6
- b_in: bfloat16 [2, 24576, 1024], P('dp', 'seq', 'head'), may hold values from -6 to 6
- c_in: bfloat16 [2, 24576, 1024], P('dp', 'seq', 'head'), may hold values from -6 to 6
- z_in: bfloat16 [2, 24576, 4096], P('dp', 'seq', 'head'), may hold values from -24 to 24
- dt_in: float32 [2, 64, 24576], P('dp', 'head', 'seq'), may hold values from -10 to 4.5
- a_log: float32 [64], P('head'), may hold values from -2.3 to 0.58
- skip_gain: float32 [64], P('head'), may hold values from 0.5 to 1.5
- norm_gain: float32 [4096], P('head'), may hold values from 0.5 to 1.5
- conv_x: float32 [4, 4096], P(None, 'head'), may hold values from -3 to 3
- conv_b: float32 [4, 1024], P(None, 'head'), may hold values from -3 to 3
- conv_c: float32 [4, 1024], P(None, 'head'), may hold values from -3 to 3
- init_state: float32 [2, 64, 64, 128], P('dp', 'head'), may hold values from -0.5 to 0.5
- out_weight: bfloat16 [4096, 8192], P(('dp', 'seq'), 'head'), may hold values from -0.09375 to 0.09375
Outputs:
- mixed: bfloat16 [2, 24576, 8192], P('dp', 'seq', 'head')
All inputs are finite; a program needn't handle non-finite values.
Results may differ from a plain program's by a relative error of at most 0.0058.
Values may be sent and summed in bfloat16 or wider, within the bound.
No kernel may reach another device: no remote copies, remote signals or barrier semaphores. Data moves between devices by JAX's collectives and lax.ppermute only.
A program may use at most 128 MiB of HBM per device.

v0:
```python
import jax
import jax.numpy as jnp
from jax import lax
from jax.sharding import PartitionSpec as P

HEAD_SIZE = 64
STATE = 128
BLOCK_LEN = 256
TAPS = 4
EPSILON = 1e-05


def from_behind(block, axis, distance):
    devices = range(lax.axis_size(axis))
    route = [(i - distance, i) for i in devices if i - distance in devices]
    return lax.ppermute(block, axis, route)


def entering(value, axis, join, neutral):
    count, mine = (lax.axis_size(axis), lax.axis_index(axis))
    pieces = jax.tree.map(lambda part: lax.all_gather(part, axis), value)
    subtotal = jax.tree.map(
        lambda part, zero: jnp.full_like(part, 0) + jnp.asarray(zero, part.dtype), value, neutral
    )

    def step(position, subtotal):
        longer = join(subtotal, jax.tree.map(lambda part: part[position], pieces))
        return jax.tree.map(lambda new, old: jnp.where(position < mine, new, old), longer, subtotal)

    return lax.fori_loop(0, count - 1, step, subtotal)


def causal_conv(signal, before, weight):
    joined = jnp.concatenate([before, signal], axis=1).astype(jnp.float32)
    length = signal.shape[1]
    tap_count = weight.shape[0]
    accum_total = weight[0] * joined[:, 0:length]
    for offset in range(1, tap_count):
        accum_total = accum_total + weight[offset] * joined[:, offset : offset + length]
    return jax.nn.silu(accum_total).astype(jnp.bfloat16)


def combine_states(first_pair, second_pair):
    return (
        first_pair[0] * second_pair[0],
        second_pair[0][..., None, None] * first_pair[1] + second_pair[1],
    )


def local(
    x_in,
    b_in,
    c_in,
    z_in,
    dt_in,
    a_log,
    skip_gain,
    norm_gain,
    conv_x,
    conv_b,
    conv_c,
    init_state,
    out_weight,
):
    highest = lax.Precision.HIGHEST
    roll_count, tok_count, wide_x = x_in.shape
    wide_b = b_in.shape[2]
    head_count = dt_in.shape[1]
    group_count = wide_b // STATE
    per_group = head_count // group_count
    block_count = tok_count // BLOCK_LEN
    rim_width = TAPS - 1
    edge_rows = jnp.concatenate(
        [
            x_in[:, tok_count - rim_width :],
            b_in[:, tok_count - rim_width :],
            c_in[:, tok_count - rim_width :],
        ],
        axis=2,
    )
    before = from_behind(edge_rows, "seq", 1)
    x_conv = causal_conv(x_in, before[:, :, :wide_x], conv_x)
    b_conv = causal_conv(b_in, before[:, :, wide_x : wide_x + wide_b], conv_b)
    c_conv = causal_conv(c_in, before[:, :, wide_x + wide_b :], conv_c)
    grouped = (roll_count, group_count, per_group, block_count, BLOCK_LEN)
    step_flat = jax.nn.softplus(dt_in)
    decay_rate = -jnp.exp(a_log)
    cum_decay = jnp.cumsum((step_flat * decay_rate[None, :, None]).reshape(grouped), axis=-1)
    step_size = step_flat.reshape(grouped)
    x_shaped = x_conv.reshape(roll_count, block_count, BLOCK_LEN, group_count, per_group, HEAD_SIZE)
    b_shaped = b_conv.reshape(roll_count, block_count, BLOCK_LEN, group_count, STATE)
    c_shaped = c_conv.reshape(roll_count, block_count, BLOCK_LEN, group_count, STATE)
    scores = jnp.einsum(
        "rcqgn,rcsgn->rgcqs", c_shaped, b_shaped, preferred_element_type=jnp.float32
    )
    query_pos = lax.broadcasted_iota(jnp.int32, (BLOCK_LEN, BLOCK_LEN), 0)
    key_pos = lax.broadcasted_iota(jnp.int32, (BLOCK_LEN, BLOCK_LEN), 1)
    causal = query_pos >= key_pos
    spread = cum_decay[..., :, None] - cum_decay[..., None, :]
    decay_mat = jnp.where(causal, jnp.exp(jnp.minimum(spread, 0.0)), jnp.float32(0.0))
    mixing = (scores[:, :, None] * decay_mat * step_size[..., None, :]).astype(jnp.bfloat16)
    intra_out = jnp.einsum(
        "rgkcqs,rcsgkp->rcqgkp", mixing, x_shaped, preferred_element_type=jnp.float32
    )
    last_decay = cum_decay[..., -1:]
    weights_in = jnp.exp(last_decay - cum_decay) * step_size
    weighted = (
        jnp.transpose(weights_in, (0, 3, 4, 1, 2))[..., None] * x_shaped.astype(jnp.float32)
    ).astype(jnp.bfloat16)
    block_states = jnp.einsum(
        "rcsgkp,rcsgn->rgkcpn", weighted, b_shaped, preferred_element_type=jnp.float32
    )
    block_decay = jnp.exp(last_decay[..., 0])
    running = jnp.zeros((roll_count, group_count, per_group, HEAD_SIZE, STATE), jnp.float32)
    carried = jnp.ones((roll_count, group_count, per_group), jnp.float32)
    starts = []
    factors = []
    for block_index in range(block_count):
        starts.append(running)
        factors.append(carried)
        running = (
            block_decay[..., block_index, None, None] * running + block_states[:, :, :, block_index]
        )
        carried = carried * block_decay[..., block_index]
    prefix_decay, prefix_state = entering(
        (carried, running), "seq", combine_states, (jnp.ones_like(carried), jnp.zeros_like(running))
    )
    incoming = prefix_state + prefix_decay[..., None, None] * init_state.reshape(
        roll_count, group_count, per_group, HEAD_SIZE, STATE
    )
    start_states = jnp.stack(
        [
            factors[block_index][..., None, None] * incoming + starts[block_index]
            for block_index in range(block_count)
        ],
        axis=3,
    )
    c_float = c_shaped.astype(jnp.float32)
    inter_out = jnp.einsum("rcqgn,rgkcpn->rcqgkp", c_float, start_states, precision=highest)
    inter_out = inter_out * jnp.transpose(jnp.exp(cum_decay), (0, 3, 4, 1, 2))[..., None]
    skip_shaped = skip_gain.reshape(group_count, per_group)[:, :, None]
    ssm_out = (intra_out + inter_out + skip_shaped * x_shaped.astype(jnp.float32)).reshape(
        roll_count, tok_count, group_count, per_group * HEAD_SIZE
    )
    gate_act = jax.nn.silu(z_in.astype(jnp.float32)).reshape(
        roll_count, tok_count, group_count, per_group * HEAD_SIZE
    )
    gated_out = ssm_out * gate_act
    mean_sq = jnp.mean(gated_out * gated_out, axis=-1, keepdims=True)
    normed = (
        gated_out
        * lax.rsqrt(mean_sq + EPSILON)
        * norm_gain.reshape(group_count, per_group * HEAD_SIZE)
    )
    normed = normed.astype(jnp.bfloat16).reshape(roll_count * tok_count, wide_x)
    wide_all = lax.all_gather(normed, "head", axis=1, tiled=True)
    full_weight = lax.all_gather(out_weight, ("dp", "seq"), axis=0, tiled=True)
    mixed_terms = jnp.dot(wide_all, full_weight, preferred_element_type=jnp.float32)
    return mixed_terms.astype(jnp.bfloat16).reshape(roll_count, tok_count, -1)


def solution(mesh):
    in_specs = (
        P("dp", "seq", "head"),
        P("dp", "seq", "head"),
        P("dp", "seq", "head"),
        P("dp", "seq", "head"),
        P("dp", "head", "seq"),
        P("head"),
        P("head"),
        P("head"),
        P(None, "head"),
        P(None, "head"),
        P(None, "head"),
        P("dp", "head", None, None),
        P(("dp", "seq"), "head"),
    )
    out_specs = P("dp", "seq", "head")
    return jax.shard_map(local, mesh=mesh, in_specs=in_specs, out_specs=out_specs, check_vma=False)
```

profile of v0, /device:TPU:65, one launch (start us, length us, event | category | flops | bytes accessed | tf_op | source)
XLA Modules:
  0.0 390.5 jit_solution(8210310024297503800)
XLA Ops:
  9.6 3.7 collective-permute-start
  14.9 3.4 reduce-window.6
  22.2 1.7 copy.154
  26.1 3.5 multiply_convert_fusion.3
  29.7 2.1 reshape.545
  33.5 2.6 multiply_convert_fusion.2
  38.9 2.6 copy.182
  41.5 3.9 convert_multiply_fusion
  45.5 5.9 %reshape.560 = f32[1,3,256,2,8,64]{2,1,5,4,3,0:T(4,128)} reshape(f32[1,768,1024]{1,2,0:T(8,128)} %convert_multiply_fusion) | data formatting | bytes 6291456 | tf_op jit(solution)/shard_map/reshape | solution.py:145
  52.1 25.1 %all-gather = f32[32,2,8,1]{2,1,3,0:T(2,128)} all-gather(f32[1,2,8,1]{2,1,3,0:T(2,128)S(1)} %copy-done.18), channel_id=2, replica_groups=mesh['dp'=2,'seq'=32,'head'=4] {'seq'}, dimensions={0}, use_global_device_ids=true | all-gather | bytes 2112 | tf_op jit(solution)/shard_map/all_gather | solution.py:21
  78.5 5.7 %reshape.562 = f32[1,3,256,2,8,64]{2,1,5,4,3,0:T(4,128)} reshape(bf16[1,768,1024]{1,2,0:T(8,128)(2,1)} %copy-done.1) | data formatting | bytes 4718592 | tf_op jit(solution)/shard_map/convert_element_type | solution.py:108
  85.7 1.6 fusion.44
  87.2 7.5 %fusion.1 = f32[3,2,8,64,256]{4,3,2,1,0:T(8,128)} fusion(f32[2,3,256,256]{3,2,0,1:T(8,128)} %fusion.44, pred[256,256]{1,0:T(8,128)(4,1)S(1)} %iota_compare_fusion, bf16[3,256,2,8,64]{1,0,4,3,2:T(4,128)(2,1)} %reshape.545, f32[2,8,3,256]{3,1,2,0:T(8,128)S(1)} %bitcast.161, f32[2,8,3,256]{3,1,2,0:T(8,128)S(1)} %copy-done.8), kind=kOutput, calls=%fused_computation.5 | convolution fusion | flops 421527552 | bytes 6455296 | tf_op jit(solution)/shard_map/rgkcqs,rcsgkp->rcqgkp/dot_general | solution.py:102
  94.7 22.5 %all-gather.5.cloned.1.call-done = f32[32,1,2,8,64,128]{5,4,3,2,1,0:T(8,128)} async-done(((f32[1,1,2,8,64,128]{5,4,3,2,1,0:T(8,128)}), f32[32,1,2,8,64,128]{5,4,3,2,1,0:T(8,128)}) %all-gather.5.cloned.1.call-update) | async-done | bytes 16777232 | tf_op jit(solution)/shard_map/all_gather | solution.py:21
  117.3 78.2 %while.16 = (s32[]{:T(128)}, f32[1,2,8]{2,1,0:T(2,128)S(1)}, f32[1,2,8,64,128]{4,3,2,1,0:T(8,128)S(1)}, s32[]{:T(128)}, f32[32,1,2,8]{3,2,1,0:T(2,128)}, /*index...) while((s32[]{:T(128)}, f32[1,2,8]{2,1,0:T(2,128)S(1)}, ...), condition=%wide.region_3.4_spmd.clone, body=%wide.region_2.3_spmd.clone.sunk | while | flops 524340 | bytes 1573367 | solution.py:30
  150.7 1.2 fusion.59
  160.8 1.2 fusion.59
  195.9 1.8 copy-done.2
  197.7 4.8 %fusion.19 = (f32[3,256,2]{1,2,0:T(2,128)S(1)}, f32[1,3,256,2,8,64]{2,5,4,3,1,0:T(8,128)S(1)}) fusion(f32[1,3,256,2,8,64]{2,1,5,4,3,0:T(4,128)S(1)} %copy-done.2, f32[1,3,256,2,8,64]{2,1,5,4,3,0:T(4,128)} %reshape.562, f32[2,8]{1,0:T(2,128)S(1)} %copy-done.15, f32[3,256,2,8]{1,3,2,0:T(8,128)S(1)} %bitcast.163, ...), kind=kOutput, calls=%fused_computation.35 | convolution fusion | flops 1214249472 | bytes 14604352 | tf_op jit(solution)/shard_map/rcqgn,rgkcpn->rcqgkp/dot_general | solution.py:139
  202.5 2.2 copy.181
  206.1 2.2 fusion.17
  208.4 34.6 %all-gather.9.cloned.1.call-done = bf16[4096,2048]{1,0:T(8,128)(2,1)} async-done(((bf16[64,2048]{1,0:T(8,128)(2,1)}), bf16[4096,2048]{1,0:T(8,128)(2,1)}) %all-gather.9.cloned.1.call-update) | async-done | bytes 16777232 | tf_op jit(solution)/shard_map/all_gather | solution.py:157
  243.0 121.2 %all-gather.7.cloned.1.call-done = bf16[768,4096]{0,1:T(8,128)(2,1)} async-done(((bf16[768,1024]{0,1:T(8,128)(2,1)}), bf16[768,4096]{0,1:T(8,128)(2,1)}) %all-gather.7.cloned.1.call-update) | async-done | bytes 6291472 | tf_op jit(solution)/shard_map/all_gather | solution.py:156
  364.2 19.8 %fusion.20 = bf16[1,768,2048]{2,1,0:T(8,128)(2,1)} fusion(bf16[768,4096]{0,1:T(8,128)(2,1)} %all-gather.7.cloned.1.call-done, bf16[4096,2048]{1,0:T(8,128)(2,1)} %all-gather.9.cloned.1.call-done), kind=kOutput, calls=%fused_computation.38 | convolution fusion | flops 12886474752 | bytes 26214400 | tf_op jit(solution)/shard_map/dot_general | solution.py:158
  (195 shorter events, 96.0 us)
Async XLA Ops:
  6.5 110.7 %all-gather.5.cloned.1.call-start = ((), (), s32[]{:S(2)}) async-start(), calls=%async_computation | async-start | bytes 17301504 | tf_op jit(solution)/shard_map/all_gather | solution.py:21
  9.6 14.8 %collective-permute-start = (bf16[1,3,1536]{1,2,0:T(8,128)(2,1)}, bf16[1,3,1536]{1,2,0:T(8,128)(2,1)}, u32[]{:S(2)}, u32[]{:S(2)}) collective-permute-start(bf16[1,3,1536]{1,2,0:T(8,128)(2,1)} %copy.153), channel_id=1, source_target_pairs={{0,4},{4,8},{8,12},{12,16},{16,20},{20,24},{24,28},{28,32},{32,36}... | collective-permute-start | bytes 27656 | tf_op jit(solution)/shard_map/ppermute | solution.py:16
  14.8 5.7 %copy-start.12 = (f32[4,1024]{1,0:T(4,128)S(1)}, f32[4,1024]{1,0:T(4,128)}, u32[]{:S(2)}) copy-start(f32[4,1024]{1,0:T(4,128)} %param.23) | copy-start | bytes 49156
  14.8 5.7 %copy-start.19 = (f32[4,256]{1,0:T(4,128)S(1)}, f32[4,256]{1,0:T(4,128)}, u32[]{:S(2)}) copy-start(f32[4,256]{1,0:T(4,128)} %param.24) | copy-start | bytes 12292
  18.6 3.1 copy-start.6
  21.1 15.5 %copy-start.13 = (f32[2,8]{1,0:T(2,128)}, f32[2,8]{1,0:T(2,128)S(1)}, u32[]{:S(2)}) copy-start(f32[2,8]{1,0:T(2,128)S(1)} %get-tuple-element.212) | copy-start | bytes 196
  22.2 14.4 %copy-start.10 = (f32[2,8]{1,0:T(2,128)}, f32[2,8]{1,0:T(2,128)S(1)}, u32[]{:S(2)}) copy-start(f32[2,8]{1,0:T(2,128)S(1)} %get-tuple-element.209) | copy-start | bytes 196
  29.6 3.7 copy-start.1
  29.7 3.1 copy-start.4
  37.7 205.3 %all-gather.9.cloned.1.call-start = ((), (), s32[]{:S(2)}) async-start(), calls=%async_computation.2 | async-start | bytes 17039360 | tf_op jit(solution)/shard_map/all_gather | solution.py:157
  38.5 325.7 %all-gather.7.cloned.1.call-start = ((), (), s32[]{:S(2)}) async-start(), calls=%async_computation.1 | async-start | bytes 7864320 | tf_op jit(solution)/shard_map/all_gather | solution.py:156
  45.4 6.0 %copy-start.22 = (f32[16]{0:T(128)S(1)}, f32[16]{0:T(128)}, u32[]{:S(2)}) copy-start(f32[16]{0:T(128)} %param.21) | copy-start | bytes 196
  45.4 6.6 %copy-start.18 = (f32[1,2,8,1]{2,1,3,0:T(2,128)S(1)}, f32[1,2,8,1]{2,1,3,0:T(2,128)}, u32[]{:S(2)}) copy-start(f32[1,2,8,1]{2,1,3,0:T(2,128)} %get-tuple-element.211) | copy-start | bytes 196
  45.4 31.7 %copy-start.20 = (f32[4,256]{1,0:T(4,128)S(1)}, f32[4,256]{1,0:T(4,128)}, u32[]{:S(2)}) copy-start(f32[4,256]{1,0:T(4,128)} %param.25) | copy-start | bytes 12292
  45.4 32.3 %copy-start.7 = (f32[2,8,3,2]{1,3,2,0:T(2,128)S(1)}, f32[2,8,3,2]{1,3,2,0:T(2,128)}, u32[]{:S(2)}) copy-start(f32[2,8,3,2]{1,3,2,0:T(2,128)} %copy-done.6) | copy-start | bytes 1156
  51.4 32.9 %copy-start.5 = (bf16[1,768,256]{2,1,0:T(8,128)(2,1)S(1)}, bf16[1,768,256]{2,1,0:T(8,128)(2,1)}, u32[]{:S(2)}) copy-start(bf16[1,768,256]{2,1,0:T(8,128)(2,1)} %param.17) | copy-start | bytes 1179652
  84.4 2.9 copy-start.8
  87.2 30.0 %copy-start.9 = (f32[1,2,8]{2,1,0:T(2,128)S(1)}, f32[1,2,8]{2,1,0:T(2,128)}, u32[]{:S(2)}) copy-start(f32[1,2,8]{2,1,0:T(2,128)} %custom-call) | copy-start | bytes 196
  117.3 78.2 %copy-start.3 = (f32[1,16,64,128]{3,2,1,0:T(8,128)S(1)}, f32[1,16,64,128]{3,2,1,0:T(8,128)}, u32[]{:S(2)}) copy-start(f32[1,16,64,128]{3,2,1,0:T(8,128)} %param.26) | copy-start | bytes 1572868
  117.3 78.2 %copy-start.11 = (f32[2,8]{1,0:T(2,128)S(1)}, f32[2,8]{1,0:T(2,128)}, u32[]{:S(2)}) copy-start(f32[2,8]{1,0:T(2,128)} %copy-done.10) | copy-start | bytes 196
  117.3 78.2 %copy-start.16 = (f32[2,8]{1,0:T(2,128)S(1)}, f32[2,8]{1,0:T(2,128)}, u32[]{:S(2)}) copy-start(f32[2,8]{1,0:T(2,128)} %get-tuple-element.213) | copy-start | bytes 196
  117.3 78.4 %copy-start.14 = (f32[2,8]{1,0:T(2,128)S(1)}, f32[2,8]{1,0:T(2,128)}, u32[]{:S(2)}) copy-start(f32[2,8]{1,0:T(2,128)} %copy-done.13) | copy-start | bytes 196
  117.3 78.4 %copy-start.17 = (f32[2,8]{1,0:T(2,128)S(1)}, f32[2,8]{1,0:T(2,128)}, u32[]{:S(2)}) copy-start(f32[2,8]{1,0:T(2,128)} %get-tuple-element.208) | copy-start | bytes 196
  195.5 2.3 copy-start.15
  (3 other events, 5.2 us)
Sparse Core Ops, SparseCore 0:
  37.8 79.3 all-gather.4
  119.1 123.8 all-gather.8
  244.8 119.2 all-gather.6
where the time goes:
time: 394 us; the launch traced here: 390 us
  waiting for transfers between devices  179 us (45%)
  other arithmetic  81.8 us (21%)
  local copies, waits for them, and re-layouts  53 us (13%)
  matrix products  34.2 us (9%)
  blocking collectives  25.1 us (6%)
  between operations  13.6 us (3%)
    all_gather x1, waiting for transfers between devices, local(): wide_all = lax.all_gather(normed, 'head', axis=1, tiled=True)  121 us
    select_n x62, other arithmetic, step(): jnp.where(position < mine, new, old)  57.5 us
    all_gather x1, waiting for transfers between devices, local(): full_weight = lax.all_gather(out_weight, ('dp', 'seq'), axis=0, tiled=True)  34.6 us
    all_gather x1, blocking collectives, entering(): pieces = jax.tree.map(lambda part: lax.all_gather(part, axis), value)  25.1 us
    all_gather x1, waiting for transfers between devices, entering(): pieces = jax.tree.map(lambda part: lax.all_gather(part, axis), value)  22.5 us
    mul x31, local copies, waits for them, and re-layouts, combine_states(): second_pair[0][..., None, None] * first_pair[1] + second_pair[1]  20.5 us
    dot_general x1, matrix products, local(): jnp.dot(wide_all, full_weight, preferred_element_type=jnp.float32)  19.8 us
  transfers between devices with their start and end apart: 4, of which 3 were waited for; matrix products, arithmetic and copies ran while one was open for 33% of the time, Pallas kernels for 0%

commit v1 on v0

--- a/solution.py
+++ b/solution.py
@@ -2,6 +2,7 @@
 import jax.numpy as jnp
 from jax import lax
 from jax.sharding import PartitionSpec as P
+from jax.lax import all_to_all, axis_size
 
 HEAD_SIZE = 64
 STATE = 128
@@ -153,7 +154,15 @@
         * norm_gain.reshape(group_count, per_group * HEAD_SIZE)
     )
     normed = normed.astype(jnp.bfloat16).reshape(roll_count * tok_count, wide_x)
-    wide_all = lax.all_gather(normed, "head", axis=1, tiled=True)
+    wide_all = jnp.concatenate(
+        all_to_all(
+            jnp.stack([normed for _ in range(axis_size("head"))], axis=0),
+            axis_name="head",
+            split_axis=0,
+            concat_axis=0,
+        ),
+        axis=1,
+    )
     full_weight = lax.all_gather(out_weight, ("dp", "seq"), axis=0, tiled=True)
     mixed_terms = jnp.dot(wide_all, full_weight, preferred_element_type=jnp.float32)
     return mixed_terms.astype(jnp.bfloat16).reshape(roll_count, tok_count, -1)

time: 394 us -> 404 us (1.025)
  waiting for transfers between devices: 179 us -> 168 us
  local copies, waits for them, and re-layouts: 53 us -> 62.6 us
  starting transfers between devices: 3.75 us -> 10.6 us
    all_gather x1 -> x0, waiting for transfers between devices: 121 us -> none  [local(): wide_all = lax.all_gather(normed, 'head', axis=1, tiled=True)]
    all_to_all x0 -> x1, waiting for transfers between devices: none -> 90.1 us  [local(): all_to_all(jnp.stack([normed for _ in range(axis_size('head'))], axis=0),...]
    all_gather x1, waiting for transfers between devices: 34.6 us -> 54.7 us  [local(): full_weight = lax.all_gather(out_weight, ('dp', 'seq'), axis=0, tiled=True)]
    all_to_all x0 -> x1, starting transfers between devices: none -> 6.88 us  [local(): all_to_all(jnp.stack([normed for _ in range(axis_size('head'))], axis=0),...]
    reshape x1 -> x2, local copies, waits for them, and re-layouts: 0.01 us -> 6.18 us  [the longest x1 6.17 us: local(): (intra_out + inter_out + skip_shaped * x_shaped.astype(jnp.float32)).resh...]
  transfers between devices with their start and end apart: 4 -> 4, of which waited for: 3 -> 3; matrix products, arithmetic and copies ran while one was open for 33% -> 36% of each run, Pallas kernels for 0% -> 0%
where the time goes in v1:
time: 404 us; the launch traced here: 397 us
  waiting for transfers between devices  168 us (42%)
  other arithmetic  82.5 us (20%)
  local copies, waits for them, and re-layouts  62.6 us (15%)
  matrix products  34.2 us (8%)
  blocking collectives  25 us (6%)
  between operations  13.8 us (3%)
  starting transfers between devices  10.6 us (3%)
    all_to_all x1, waiting for transfers between devices, local(): all_to_all(jnp.stack([normed for _ in range(axis_size('head'))], axis=0),...  90.1 us
    select_n x62, other arithmetic, step(): jnp.where(position < mine, new, old)  57.3 us
    all_gather x1, waiting for transfers between devices, local(): full_weight = lax.all_gather(out_weight, ('dp', 'seq'), axis=0, tiled=True)  54.7 us
    all_gather x1, blocking collectives, entering(): pieces = jax.tree.map(lambda part: lax.all_gather(part, axis), value)  25 us
    all_gather x1, waiting for transfers between devices, entering(): pieces = jax.tree.map(lambda part: lax.all_gather(part, axis), value)  22.7 us
    mul x31, local copies, waits for them, and re-layouts, combine_states(): second_pair[0][..., None, None] * first_pair[1] + second_pair[1]  20.5 us
    dot_general x1, matrix products, local(): jnp.dot(wide_all, full_weight, preferred_element_type=jnp.float32)  19.8 us
  transfers between devices with their start and end apart: 4, of which 3 were waited for; matrix products, arithmetic and copies ran while one was open for 36% of the time, Pallas kernels for 0%

profile of v1, /device:TPU:65, one launch (start us, length us, event | category | flops | bytes accessed | tf_op | source)
XLA Modules:
  0.0 397.1 jit_solution(3130618944018072615)
XLA Ops:
  9.6 3.7 collective-permute-start
  14.9 3.4 reduce-window.6
  22.3 1.7 copy.154
  26.2 3.5 multiply_convert_fusion.3
  29.7 2.1 reshape.550
  33.5 2.6 multiply_convert_fusion.2
  38.9 2.6 copy.182
  41.5 3.9 convert_multiply_fusion
  45.4 5.9 %reshape.564 = f32[1,3,256,2,8,64]{2,1,5,4,3,0:T(4,128)} reshape(f32[1,768,1024]{1,2,0:T(8,128)} %convert_multiply_fusion) | data formatting | bytes 6291456 | tf_op jit(solution)/shard_map/reshape | solution.py:146
  52.0 25.0 %all-gather = f32[32,2,8,1]{2,1,3,0:T(2,128)} all-gather(f32[1,2,8,1]{2,1,3,0:T(2,128)S(1)} %copy-done.18), channel_id=2, replica_groups=mesh['dp'=2,'seq'=32,'head'=4] {'seq'}, dimensions={0}, use_global_device_ids=true | all-gather | bytes 2112 | tf_op jit(solution)/shard_map/all_gather | solution.py:22
  78.4 5.7 %reshape.568 = f32[1,3,256,2,8,64]{2,1,5,4,3,0:T(4,128)} reshape(bf16[1,768,1024]{1,2,0:T(8,128)(2,1)} %copy-done.1) | data formatting | bytes 4718592 | tf_op jit(solution)/shard_map/convert_element_type | solution.py:109
  87.1 7.5 %fusion.1 = f32[3,2,8,64,256]{4,3,2,1,0:T(8,128)} fusion(f32[2,3,256,256]{3,2,0,1:T(8,128)} %fusion.44, pred[256,256]{1,0:T(8,128)(4,1)S(1)} %iota_compare_fusion, bf16[3,256,2,8,64]{1,0,4,3,2:T(4,128)(2,1)} %reshape.550, f32[2,8,3,256]{3,1,2,0:T(8,128)S(1)} %bitcast.157, f32[2,8,3,256]{3,1,2,0:T(8,128)S(1)} %copy-done.8), kind=kOutput, calls=%fused_computation.5 | convolution fusion | flops 421527552 | bytes 6455296 | tf_op jit(solution)/shard_map/rgkcqs,rcsgkp->rcqgkp/dot_general | solution.py:103
  94.6 22.7 %all-gather.4.cloned.1.call-done = f32[32,1,2,8,64,128]{5,4,3,2,1,0:T(8,128)} async-done(((f32[1,1,2,8,64,128]{5,4,3,2,1,0:T(8,128)}), f32[32,1,2,8,64,128]{5,4,3,2,1,0:T(8,128)}) %all-gather.4.cloned.1.call-update) | async-done | bytes 16777232 | tf_op jit(solution)/shard_map/all_gather | solution.py:22
  117.4 78.0 %while.16 = (s32[]{:T(128)}, f32[1,2,8]{2,1,0:T(2,128)S(1)}, f32[1,2,8,64,128]{4,3,2,1,0:T(8,128)S(1)}, s32[]{:T(128)}, f32[32,1,2,8]{3,2,1,0:T(2,128)}, /*index...) while((s32[]{:T(128)}, f32[1,2,8]{2,1,0:T(2,128)S(1)}, ...), condition=%wide.region_3.4_spmd.clone, body=%wide.region_2.3_spmd.clone.sunk | while | flops 524340 | bytes 1573367 | solution.py:31
  195.7 1.8 copy-done.2
  197.6 4.8 %fusion.19 = (f32[3,256,2]{1,2,0:T(2,128)S(1)}, f32[1,3,256,2,8,64]{2,5,4,3,1,0:T(8,128)S(1)}) fusion(f32[1,3,256,2,8,64]{2,1,5,4,3,0:T(4,128)S(1)} %copy-done.2, f32[1,3,256,2,8,64]{2,1,5,4,3,0:T(4,128)} %reshape.568, f32[2,8]{1,0:T(2,128)S(1)} %copy-done.15, f32[3,256,2,8]{1,3,2,0:T(8,128)S(1)} %bitcast.159, ...), kind=kOutput, calls=%fused_computation.34 | convolution fusion | flops 1214249472 | bytes 14604352 | tf_op jit(solution)/shard_map/rcqgn,rgkcpn->rcqgkp/dot_general | solution.py:140
  202.4 4.1 %copy.181 = f32[1,3,256,2,8,64]{2,1,5,4,3,0:T(4,128)} copy(f32[1,3,256,2,8,64]{2,5,4,3,1,0:T(8,128)S(1)} %get-tuple-element.215) | data formatting | bytes 6291456 | tf_op jit(solution)/shard_map/add | solution.py:143
  206.5 6.2 %reshape.563 = f32[1,768,1024]{1,2,0:T(8,128)} reshape(f32[1,3,256,2,8,64]{2,1,5,4,3,0:T(4,128)} %copy.181) | data formatting | bytes 6291456 | tf_op jit(solution)/shard_map/reshape | solution.py:143
  212.7 3.0 fusion.17
  215.8 3.0 stack.19
  218.8 6.9 %all-to-all-start = ((bf16[4,768,1024]{1,2,0:T(8,128)(2,1)}), bf16[4,768,1024]{1,2,0:T(8,128)(2,1)}, u32[]{:S(2)}, u32[]{:S(2)}) async-start(bf16[4,768,1024]{1,2,0:T(8,128)(2,1)} %stack.19), calls=%async_computation | async-start | bytes 12582912 | tf_op jit(solution)/shard_map/all_to_all | solution.py:158
  225.7 54.7 %all-gather.6.cloned.1.call-done = bf16[4096,2048]{1,0:T(8,128)(2,1)} async-done(((bf16[64,2048]{1,0:T(8,128)(2,1)}), bf16[4096,2048]{1,0:T(8,128)(2,1)}) %all-gather.6.cloned.1.call-update) | async-done | bytes 16777232 | tf_op jit(solution)/shard_map/all_gather | solution.py:166
  280.4 90.1 %all-to-all-done = bf16[4,768,1024]{1,2,0:T(8,128)(2,1)} async-done(((bf16[4,768,1024]{1,2,0:T(8,128)(2,1)}), bf16[4,768,1024]{1,2,0:T(8,128)(2,1)}, u32[]{:S(2)}, u32[]{:S(2)}) %all-to-all-start) | async-done | bytes 6291488 | tf_op jit(solution)/shard_map/all_to_all | solution.py:158
  370.4 19.8 %fusion.20 = bf16[1,768,2048]{2,1,0:T(8,128)(2,1)} fusion(bf16[768,4096]{0,1:T(8,128)(2,1)} %bitcast.54, bf16[4096,2048]{1,0:T(8,128)(2,1)} %all-gather.6.cloned.1.call-done), kind=kOutput, calls=%fused_computation.37 | convolution fusion | flops 12886474752 | bytes 26214400 | tf_op jit(solution)/shard_map/dot_general | solution.py:167
  (195 shorter events, 98.3 us)
Async XLA Ops:
  6.5 110.8 %all-gather.4.cloned.1.call-start = ((), (), s32[]{:S(2)}) async-start(), calls=%async_computation.1 | async-start | bytes 17301504 | tf_op jit(solution)/shard_map/all_gather | solution.py:22
  9.6 14.8 %collective-permute-start = (bf16[1,3,1536]{1,2,0:T(8,128)(2,1)}, bf16[1,3,1536]{1,2,0:T(8,128)(2,1)}, u32[]{:S(2)}, u32[]{:S(2)}) collective-permute-start(bf16[1,3,1536]{1,2,0:T(8,128)(2,1)} %copy.153), channel_id=1, source_target_pairs={{0,4},{4,8},{8,12},{12,16},{16,20},{20,24},{24,28},{28,32},{32,36}... | collective-permute-start | bytes 27656 | tf_op jit(solution)/shard_map/ppermute | solution.py:17
  14.8 5.7 %copy-start.12 = (f32[4,1024]{1,0:T(4,128)S(1)}, f32[4,1024]{1,0:T(4,128)}, u32[]{:S(2)}) copy-start(f32[4,1024]{1,0:T(4,128)} %param.23) | copy-start | bytes 49156
  14.8 5.7 %copy-start.19 = (f32[4,256]{1,0:T(4,128)S(1)}, f32[4,256]{1,0:T(4,128)}, u32[]{:S(2)}) copy-start(f32[4,256]{1,0:T(4,128)} %param.24) | copy-start | bytes 12292
  18.6 3.1 copy-start.6
  21.1 15.6 %copy-start.13 = (f32[2,8]{1,0:T(2,128)}, f32[2,8]{1,0:T(2,128)S(1)}, u32[]{:S(2)}) copy-start(f32[2,8]{1,0:T(2,128)S(1)} %get-tuple-element.212) | copy-start | bytes 196
  22.3 14.4 %copy-start.10 = (f32[2,8]{1,0:T(2,128)}, f32[2,8]{1,0:T(2,128)S(1)}, u32[]{:S(2)}) copy-start(f32[2,8]{1,0:T(2,128)S(1)} %get-tuple-element.209) | copy-start | bytes 196
  29.7 3.7 copy-start.1
  29.7 3.1 copy-start.4
  37.7 242.6 %all-gather.6.cloned.1.call-start = ((), (), s32[]{:S(2)}) async-start(), calls=%async_computation.2 | async-start | bytes 17039360 | tf_op jit(solution)/shard_map/all_gather | solution.py:166
  45.4 5.9 %copy-start.22 = (f32[16]{0:T(128)S(1)}, f32[16]{0:T(128)}, u32[]{:S(2)}) copy-start(f32[16]{0:T(128)} %param.21) | copy-start | bytes 196
  45.4 6.6 %copy-start.18 = (f32[1,2,8,1]{2,1,3,0:T(2,128)S(1)}, f32[1,2,8,1]{2,1,3,0:T(2,128)}, u32[]{:S(2)}) copy-start(f32[1,2,8,1]{2,1,3,0:T(2,128)} %get-tuple-element.211) | copy-start | bytes 196
  45.4 31.6 %copy-start.20 = (f32[4,256]{1,0:T(4,128)S(1)}, f32[4,256]{1,0:T(4,128)}, u32[]{:S(2)}) copy-start(f32[4,256]{1,0:T(4,128)} %param.25) | copy-start | bytes 12292
  45.4 32.3 %copy-start.7 = (f32[2,8,3,2]{1,3,2,0:T(2,128)S(1)}, f32[2,8,3,2]{1,3,2,0:T(2,128)}, u32[]{:S(2)}) copy-start(f32[2,8,3,2]{1,3,2,0:T(2,128)} %copy-done.6) | copy-start | bytes 1156
  51.4 32.8 %copy-start.5 = (bf16[1,768,256]{2,1,0:T(8,128)(2,1)S(1)}, bf16[1,768,256]{2,1,0:T(8,128)(2,1)}, u32[]{:S(2)}) copy-start(bf16[1,768,256]{2,1,0:T(8,128)(2,1)} %param.17) | copy-start | bytes 1179652
  87.1 30.2 %copy-start.9 = (f32[1,2,8]{2,1,0:T(2,128)S(1)}, f32[1,2,8]{2,1,0:T(2,128)}, u32[]{:S(2)}) copy-start(f32[1,2,8]{2,1,0:T(2,128)} %custom-call) | copy-start | bytes 196
  117.3 78.0 %copy-start.3 = (f32[1,16,64,128]{3,2,1,0:T(8,128)S(1)}, f32[1,16,64,128]{3,2,1,0:T(8,128)}, u32[]{:S(2)}) copy-start(f32[1,16,64,128]{3,2,1,0:T(8,128)} %param.26) | copy-start | bytes 1572868
  117.3 78.0 %copy-start.11 = (f32[2,8]{1,0:T(2,128)S(1)}, f32[2,8]{1,0:T(2,128)}, u32[]{:S(2)}) copy-start(f32[2,8]{1,0:T(2,128)} %copy-done.10) | copy-start | bytes 196
  117.3 78.0 %copy-start.16 = (f32[2,8]{1,0:T(2,128)S(1)}, f32[2,8]{1,0:T(2,128)}, u32[]{:S(2)}) copy-start(f32[2,8]{1,0:T(2,128)} %get-tuple-element.213) | copy-start | bytes 196
  117.4 78.2 %copy-start.14 = (f32[2,8]{1,0:T(2,128)S(1)}, f32[2,8]{1,0:T(2,128)}, u32[]{:S(2)}) copy-start(f32[2,8]{1,0:T(2,128)} %copy-done.13) | copy-start | bytes 196
  117.4 78.2 %copy-start.17 = (f32[2,8]{1,0:T(2,128)S(1)}, f32[2,8]{1,0:T(2,128)}, u32[]{:S(2)}) copy-start(f32[2,8]{1,0:T(2,128)} %get-tuple-element.208) | copy-start | bytes 196
  206.5 6.2 %copy-start = (bf16[1,768,1024]{1,2,0:T(8,128)(2,1)S(1)}, bf16[1,768,1024]{1,2,0:T(8,128)(2,1)}, u32[]{:S(2)}) copy-start(bf16[1,768,1024]{1,2,0:T(8,128)(2,1)} %copy.182) | copy-start | bytes 4718596
  206.5 6.2 %copy-start.21 = (f32[1024]{0:T(1024)S(1)}, f32[1024]{0:T(1024)}, u32[]{:S(2)}) copy-start(f32[1024]{0:T(1024)} %param.22) | copy-start | bytes 12292
  218.8 151.6 %all-to-all-start = ((bf16[4,768,1024]{1,2,0:T(8,128)(2,1)}), bf16[4,768,1024]{1,2,0:T(8,128)(2,1)}, u32[]{:S(2)}, u32[]{:S(2)}) async-start(bf16[4,768,1024]{1,2,0:T(8,128)(2,1)} %stack.19), calls=%async_computation | async-start | bytes 12582912 | tf_op jit(solution)/shard_map/all_to_all | solution.py:158
  (3 other events, 7.4 us)
Sparse Core Ops, SparseCore 0:
  37.8 79.4 all-gather.3
  119.2 161.1 all-gather.5
